TPU v7x, 32 devices: a whole 2x2x4 slice. The times are simulated.
32 devices in a mesh: groups: 2 (over x), ctx: 16 (over z, y, core).
Axes of the slice: x: 2, y: 2, z: 4, core: 2. Of those that a mesh axis runs over, the one named last changes fastest.
Arguments:
- queries: bfloat16 [12288, 1024], P(('groups', 'ctx')), parts along dimension 0
- keys: bfloat16 [12288, 1024], P(('groups', 'ctx')), parts along dimension 0
- values: bfloat16 [12288, 1024], P(('groups', 'ctx')), parts along dimension 0, may hold values from -6 to 6
- out_weight: bfloat16 [1024, 1024], P('ctx'), may hold values from -0.1875 to 0.1875
- grad_output: bfloat16 [12288, 1024], P(('groups', 'ctx')), parts along dimension 0, may hold values from -6 to 6
- complex_id: int32 [12288], P('groups'), parts along dimension 0, may hold values from 0 to 3, never falling along the last dimension, each value on 1 to 3072 neighbouring positions
- contacts: int32 [96, 6], P(('groups', 'ctx')), parts along dimension 0, may hold values from 0 to 47, as said below
- contact_count: int32 [96], P(('groups', 'ctx')), parts along dimension 0, may hold values from 3 to 6, as said below
Outputs:
- mixed: bfloat16 [12288, 1024], P(('groups', 'ctx')), parts along dimension 0
- grad_queries: bfloat16 [12288, 1024], P(('groups', 'ctx')), parts along dimension 0
- grad_keys: bfloat16 [12288, 1024], P(('groups', 'ctx')), parts along dimension 0
- grad_values: bfloat16 [12288, 1024], P(('groups', 'ctx')), parts along dimension 0
- grad_weight: float32 [2048, 1024], P(('groups', 'ctx')), parts along dimension 0
There are 2 independent parts, one for each index of `groups`. A program takes and returns all parts, laid end to end along the dimension named above; an argument that names none is the same for every part. Nothing has to cross between parts.
Inputs may be any that keep to these rules, and one draw needn't show every extreme that they name: `contacts`: entry 0 of each list is the query block itself; the other entries are distinct blocks, other than the query block, at most 6 blocks from it. `contact_count`: on some device every block of the device has all 6 entries live.
All inputs are finite; a program needn't handle non-finite values.
Results may differ from a plain program's by a relative error of at most 0.022.
Values may be sent and summed in bfloat16 or wider, within the bound.
A program may use at most 192 MiB of HBM per device.

v0:
```python
import functools
import math

import jax
import jax.numpy as jnp
from jax import lax
from jax.experimental import pallas as pl
from jax.experimental.pallas import tpu as pltpu
from jax.sharding import PartitionSpec as P

HEADS = 16
REACH_DEV = 2
LANES = 128


def neighbours(n):
    me = lax.axis_index("ctx")
    core, y = lax.rem(me, 2), lax.rem(me // 2, 2)
    ahead, behind = me + 4 - 8 * y, me - 4 + 8 * y
    has_ahead = (ahead >= 0) & (ahead < n)
    has_behind = (behind >= 0) & (behind < n)
    return core, y, me + 2 - 4 * y, me + 1 - 2 * core, ahead, behind, has_ahead, has_behind


def greet(ypeer, cpeer, ahead, behind, has_ahead, has_behind):
    barrier = pltpu.get_barrier_semaphore()

    def hello(device):
        pl.semaphore_signal(barrier, inc=1, device_id={"ctx": device}, device_id_type=pl.DeviceIdType.MESH)

    hello(ypeer)
    hello(cpeer)
    pl.when(has_ahead)(lambda: hello(ahead))
    pl.when(has_behind)(lambda: hello(behind))
    pl.semaphore_wait(barrier, 2 + has_ahead.astype(jnp.int32) + has_behind.astype(jnp.int32))


def remote(src, dst, send, recv, device):
    return pltpu.make_async_remote_copy(
        src_ref=src, dst_ref=dst, send_sem=send, recv_sem=recv,
        device_id={"ctx": device}, device_id_type=pl.DeviceIdType.MESH,
    )


def gather_kernel(n, chunks, k_ref, v_ref, kwin, vwin, sends, recvs):
    core, y, ypeer, cpeer, ahead, behind, has_ahead, has_behind = neighbours(n)
    greet(ypeer, cpeer, ahead, behind, has_ahead, has_behind)
    step = k_ref.shape[0] // chunks
    owns, wins = (k_ref, v_ref), (kwin, vwin)
    total = 2 * chunks

    def at(c):
        return c % 2, pl.ds((c // 2) * step, step)

    def over_y(c):
        a, r = at(c)
        return remote(owns[a].at[r], wins[a].at[3 * y, r], sends.at[0, c], recvs.at[0, c], ypeer)

    def over_z(c):
        a, r = at(c)
        return remote(wins[a].at[3 - 3 * y, r], wins[a].at[3 * y, r], sends.at[1, c], recvs.at[1, c], ahead)

    def across(c):
        a, r = at(c)
        return remote(owns[a].at[r], wins[a].at[1 + core, r], sends.at[2, c], recvs.at[2, c], cpeer)

    def onward(c):
        a, r = at(c)
        return remote(
            wins[a].at[3 - 3 * core, r], wins[a].at[2 - core, r], sends.at[3, c], recvs.at[3, c], cpeer
        )

    def late(c):
        pl.when(has_behind)(lambda: over_z(c).wait_recv())
        pl.when(has_behind & (y != core))(lambda: onward(c).start())

    for c in range(total):
        over_y(c).start()
    for c in range(total):
        across(c).start()
    for c in range(total):
        over_y(c).wait_recv()
        pl.when(has_ahead)(lambda c=c: over_z(c).start())
        pl.when(y == core)(lambda c=c: onward(c).start())
        if c:
            late(c - 1)
    late(total - 1)
    for c in range(total):
        over_y(c).wait_send()
        pl.when(has_ahead)(lambda c=c: over_z(c).wait_send())
        across(c).wait_send()
        across(c).wait_recv()
        pl.when((y == core) | has_behind)(lambda c=c: onward(c).wait_send())
        pl.when((y != core) | has_behind)(lambda c=c: onward(c).wait_recv())


def gather_window(keys, values, chunks=6):
    n = lax.axis_size("ctx")
    any_space = pl.BlockSpec(memory_space=pl.ANY)
    shape = jax.ShapeDtypeStruct((2 * REACH_DEV,) + keys.shape, keys.dtype)
    return pl.pallas_call(
        functools.partial(gather_kernel, n, chunks),
        out_shape=[shape, shape],
        in_specs=[any_space] * 2,
        out_specs=[any_space] * 2,
        scratch_shapes=[pltpu.SemaphoreType.DMA((4, 2 * chunks)), pltpu.SemaphoreType.DMA((4, 2 * chunks))],
        compiler_params=pltpu.CompilerParams(collective_id=0, has_side_effects=True),
        cost_estimate=pl.CostEstimate(flops=0, bytes_accessed=150_000_000, transcendentals=0),
        name="gather_window",
    )(keys, values)


def return_kernel(n, chunks, far, own, gk_ref, gv_ref, got_f, got_c, got_z, got_y, put_z, put_y, sends, recvs):
    core, y, ypeer, cpeer, ahead, behind, has_ahead, has_behind = neighbours(n)
    greet(ypeer, cpeer, ahead, behind, has_ahead, has_behind)
    step = own.shape[1] // chunks
    total = 2 * chunks
    f32, bf16 = jnp.float32, jnp.bfloat16

    def at(c):
        return c % 2, pl.ds((c // 2) * step, step)

    def back(c):
        a, r = at(c)
        return remote(far.at[1 + core, a, r], got_f.at[a, r], sends.at[0, c], recvs.at[0, c], cpeer)

    def across(c):
        a, r = at(c)
        return remote(far.at[2 - core, a, r], got_c.at[a, r], sends.at[1, c], recvs.at[1, c], cpeer)

    def over_z(c):
        a, r = at(c)
        return remote(put_z.at[a, r], got_z.at[a, r], sends.at[2, c], recvs.at[2, c], behind)

    def over_y(c):
        a, r = at(c)
        return remote(put_y.at[a, r], got_y.at[a, r], sends.at[3, c], recvs.at[3, c], ypeer)

    sent_back = (y != core) | has_behind
    got_back = (y == core) | has_behind
    for c in range(total):
        pl.when(sent_back)(lambda c=c: back(c).start())

    def second(c):
        a, r = at(c)
        pl.when(has_ahead)(lambda: over_z(c).wait_recv())
        value = far[3 - 3 * y, a, r, :].astype(f32)
        value = value + jnp.where(has_ahead, got_z[a, r, :].astype(f32), 0.0)
        value = value + jnp.where(y == core, got_f[a, r, :].astype(f32), 0.0)
        put_y[a, r, :] = value.astype(bf16)
        over_y(c).start()

    for c in range(total):
        a, r = at(c)
        pl.when(got_back)(lambda c=c: back(c).wait_recv())
        value = far[3 * y, a, r, :].astype(f32)
        put_z[a, r, :] = (value + jnp.where(y != core, got_f[a, r, :].astype(f32), 0.0)).astype(bf16)
        pl.when(has_behind)(lambda c=c: over_z(c).start())
        across(c).start()
        if c >= 2:
            second(c - 2)
    second(total - 2)
    second(total - 1)
    for c in range(total):
        a, r = at(c)
        across(c).wait_recv()
        over_y(c).wait_recv()
        value = own[a, r, :] + got_c[a, r, :].astype(f32) + got_y[a, r, :].astype(f32)
        (gk_ref, gv_ref)[a][r, :] = value.astype(bf16)
    for c in range(total):
        pl.when(sent_back)(lambda c=c: back(c).wait_send())
        across(c).wait_send()
        pl.when(has_behind)(lambda c=c: over_z(c).wait_send())
        over_y(c).wait_send()


def return_grads(far, own, chunks=6):
    n = lax.axis_size("ctx")
    _, rows, width = own.shape
    space = pl.BlockSpec(memory_space=pltpu.VMEM)
    shape = jax.ShapeDtypeStruct((rows, width), jnp.bfloat16)
    return pl.pallas_call(
        functools.partial(return_kernel, n, chunks),
        out_shape=[shape, shape],
        in_specs=[space] * 2,
        out_specs=[space] * 2,
        scratch_shapes=[pltpu.VMEM((2, rows, width), jnp.bfloat16)] * 6
        + [pltpu.SemaphoreType.DMA((4, 2 * chunks)), pltpu.SemaphoreType.DMA((4, 2 * chunks))],
        compiler_params=pltpu.CompilerParams(
            collective_id=1, has_side_effects=True, vmem_limit_bytes=56 * 1024 * 1024
        ),
        cost_estimate=pl.CostEstimate(flops=0, bytes_accessed=150_000_000, transcendentals=0),
        name="return_grads",
    )(far, own)


def attention_kernel(
    blocks, listed, block, head_dim,
    local_ref, count_ref, q_ref, k_ref, v_ref, d_ref,
    kfar, vfar, idk_ref, idq_ref,
    att_ref, dq_ref, own_ref, far_ref,
    kwin, vwin, bias, gk, gv, kg, vg,
):
    rows = blocks * block
    scale = 1.0 / math.sqrt(head_dim)
    f32, bf16 = jnp.float32, jnp.bfloat16

    @pl.when(pl.program_id(0) == 0)
    def _():
        for b in range(blocks):
            mine = idq_ref[b : b + 1, :]
            for j in range(listed):
                start = pl.multiple_of(local_ref[b, j] * block, block)
                same = idk_ref[pl.ds(start, block), :] == mine
                alive = jnp.where(j < count_ref[b], 0.0, -jnp.inf).astype(f32)
                bias[pl.ds((b * listed + j) * block, block), :] = jnp.where(same, alive, -jnp.inf)

    for i, piece in enumerate((0, 1, None, 2, 3)):
        span = pl.ds(i * rows, rows)
        kwin[span, :] = k_ref[...] if piece is None else kfar[piece]
        vwin[span, :] = v_ref[...] if piece is None else vfar[piece]
    gk[...] = jnp.zeros_like(gk)
    gv[...] = jnp.zeros_like(gv)

    lane = lax.broadcasted_iota(jnp.int32, (block, LANES), 1) < head_dim
    sub = lax.broadcasted_iota(jnp.int32, (LANES, block), 0) < head_dim
    last = (((1,), (1,)), ((), ()))
    first = (((0,), (0,)), ((), ()))

    def two(x):
        zero = jnp.zeros_like(x)
        return jnp.concatenate([jnp.where(lane, x, zero), jnp.where(lane, zero, x)], axis=0).astype(bf16)

    for b in range(blocks):
        here = pl.ds(b * block, block)
        starts = [pl.multiple_of(local_ref[b, j] * block, block) for j in range(listed)]
        for j in range(listed):
            kg[pl.ds(j * block, block), :] = kwin[pl.ds(starts[j], block), :]
            vg[pl.ds(j * block, block), :] = vwin[pl.ds(starts[j], block), :]
        grad = d_ref[here, :].astype(f32)
        q2 = two(q_ref[here, :].astype(f32) * scale)
        d2 = two(grad)
        s = lax.dot_general(kg[...], q2, last, preferred_element_type=f32)
        mask = bias[pl.ds(b * listed * block, listed * block), :]
        s = s + jnp.concatenate([mask, mask], axis=1)
        top = jnp.max(s, axis=0, keepdims=True)
        e = jnp.exp(s - top)
        probs = e * (1.0 / jnp.sum(e, axis=0, keepdims=True))
        low = probs.astype(bf16)
        ot = lax.dot_general(vg[...], low, first, preferred_element_type=f32)
        att = jnp.where(sub, ot[:, :block], ot[:, block:]).astype(bf16).astype(f32)
        att_ref[here, :] = att.T.astype(bf16)
        prod = grad.T * att
        row_dot = jnp.concatenate(
            [jnp.sum(prod[:head_dim], axis=0, keepdims=True), jnp.sum(prod[head_dim:], axis=0, keepdims=True)],
            axis=1,
        )
        dp = lax.dot_general(vg[...], d2, last, preferred_element_type=f32)
        ds = (probs * (dp - row_dot)).astype(bf16)
        dqt = lax.dot_general(kg[...], ds, first, preferred_element_type=f32)
        dq = jnp.where(sub, dqt[:, :block], dqt[:, block:]) * scale
        dq_ref[here, :] = dq.T.astype(bf16)
        dk = jnp.dot(ds, q2, preferred_element_type=f32)
        dv = jnp.dot(low, d2, preferred_element_type=f32)
        for j in range(listed):
            part = slice(j * block, (j + 1) * block)
            gk[pl.ds(starts[j], block), :] += dk[part]
            gv[pl.ds(starts[j], block), :] += dv[part]

    own = pl.ds(REACH_DEV * rows, rows)
    own_ref[0] = gk[own, :]
    own_ref[1] = gv[own, :]
    for i, at in enumerate((0, 1, 3, 4)):
        span = pl.ds(at * rows, rows)
        far_ref[i, 0] = gk[span, :].astype(bf16)
        far_ref[i, 1] = gv[span, :].astype(bf16)


def attention(local, count, queries, keys, values, grad_input, kfar, vfar, idk, idq):
    rows, width = queries.shape
    blocks, listed = local.shape
    block = rows // blocks
    head_dim = width // HEADS
    window = (2 * REACH_DEV + 1) * rows
    flat = pl.BlockSpec((rows, LANES), lambda p, *_: (0, p))
    pair = pl.BlockSpec((2, rows, LANES), lambda p, *_: (0, 0, p))
    quad = pl.BlockSpec((2 * REACH_DEV, rows, LANES), lambda p, *_: (0, 0, p))
    far = pl.BlockSpec((2 * REACH_DEV, 2, rows, LANES), lambda p, *_: (0, 0, 0, p))
    whole = lambda shape: pl.BlockSpec(shape, lambda p, *_: (0, 0))
    f32, bf16 = jnp.float32, jnp.bfloat16
    return pl.pallas_call(
        functools.partial(attention_kernel, blocks, listed, block, head_dim),
        grid_spec=pltpu.PrefetchScalarGridSpec(
            num_scalar_prefetch=2,
            grid=(width // LANES,),
            in_specs=[flat, flat, flat, flat, quad, quad, whole(idk.shape), whole(idq.shape)],
            out_specs=[flat, flat, pair, far],
            scratch_shapes=[
                pltpu.VMEM((window, LANES), bf16),
                pltpu.VMEM((window, LANES), bf16),
                pltpu.VMEM((blocks * listed * block, LANES), f32),
                pltpu.VMEM((window, LANES), f32),
                pltpu.VMEM((window, LANES), f32),
                pltpu.VMEM((listed * block, LANES), bf16),
                pltpu.VMEM((listed * block, LANES), bf16),
            ],
        ),
        out_shape=[
            jax.ShapeDtypeStruct((rows, width), bf16),
            jax.ShapeDtypeStruct((rows, width), bf16),
            jax.ShapeDtypeStruct((2, rows, width), f32),
            jax.ShapeDtypeStruct((2 * REACH_DEV, 2, rows, width), bf16),
        ],
        compiler_params=pltpu.CompilerParams(dimension_semantics=("arbitrary",)),
        name="contact_attention",
    )(local, count, queries, keys, values, grad_input, kfar, vfar, idk, idq)


def shards(queries, keys, values, out_weight, grad_output, complex_id, contacts, contact_count):
    rows, width = queries.shape
    local_blocks, listed = contacts.shape
    block = rows // local_blocks
    position = lax.axis_index("ctx")
    total_tokens = rows * lax.axis_size("ctx")
    f32, bf16 = jnp.float32, jnp.bfloat16
    weight = lax.all_gather(out_weight, "ctx", axis=0, tiled=True)
    kfar, vfar = gather_window(keys, values)
    grad_input = lax.dot_general(
        grad_output, weight, (((1,), (1,)), ((), ())), preferred_element_type=f32
    ).astype(bf16)
    margin = REACH_DEV * rows
    ids = lax.dynamic_slice_in_dim(
        jnp.pad(complex_id, (margin, margin), constant_values=-1), position * rows, rows + 2 * margin
    )
    idk = jnp.broadcast_to(ids[:, None], (rows + 2 * margin, LANES))
    idq = ids[margin : margin + rows].reshape(local_blocks, block)
    local = contacts - (position - REACH_DEV) * local_blocks
    attended, grad_queries, own, far = attention(
        local, contact_count, queries, keys, values, grad_input,
        kfar, vfar, idk, idq,
    )
    grad_keys, grad_values = return_grads(far, own)
    mixed = jnp.dot(attended, weight, preferred_element_type=f32).astype(bf16)
    grad_weight = lax.psum_scatter(
        lax.dot_general(attended, grad_output, (((0,), (0,)), ((), ())), preferred_element_type=f32),
        "ctx",
        scatter_dimension=0,
        tiled=True,
    ) * jnp.float32(1.0 / math.sqrt(total_tokens))
    return mixed, grad_queries, grad_keys, grad_values, grad_weight


def solution(mesh):
    split = P(("groups", "ctx"), None)
    return jax.shard_map(
        shards,
        mesh=mesh,
        in_specs=(split, split, split, P("ctx", None), split, P("groups"), split, P(("groups", "ctx"))),
        out_specs=(split,) * 5,
        check_vma=False,
    )
```

profile of v0, /device:TPU:20, one launch (start us, length us, event | category | flops | bytes accessed | tf_op | source)
XLA Modules:
  0.0 207.4 jit_solution(8888901730136015935)
XLA Ops:
  7.2 0.0 copy-start
  7.2 0.0 all-gather.2.cloned.1.call-start
  7.2 0.7 all-gather.2.cloned.1.call-update
  7.9 0.0 reduce-scatter.2.cloned.1.call-start
  8.0 57.3 %gather_window.1 = (bf16[4,384,1024]{2,1,0:T(8,128)(2,1)}, bf16[4,384,1024]{2,1,0:T(8,128)(2,1)}) custom-call(bf16[384,1024]{1,0:T(8,128)(2,1)} %k_ref.3, bf16[384,1024]{1,0:T(8,128)(2,1)} %v_ref.3), custom_call_target="tpu_custom_call" | custom-call | bytes 150000000 | tf_op jit(solution)/shard_map/gather_window/pallas_call | solution.py:101
  65.2 1.4 fusion.idq_ref
  66.6 0.8 pad_dynamic-slice_fusion.1
  67.4 1.3 broadcast_subtract_fusion.local_ref
  68.6 0.0 all-gather.2.cloned.1.call-done
  68.6 0.0 copy-done
  68.7 3.5 %convolution_convert_fusion.1.d_ref = bf16[384,1024]{1,0:T(8,128)(2,1)} fusion(bf16[384,1024]{1,0:T(8,128)(2,1)S(1)} %copy-done, bf16[1024,1024]{1,0:T(8,128)(2,1)} %all-gather.2.cloned.1.call-done), kind=kOutput, calls=%fused_computation.1 | convolution fusion | flops 805699584 | bytes 3670016 | tf_op jit(solution)/shard_map/dot_general | solution.py:328
  72.1 1.3 broadcast_in_dim.2.idk_ref
  73.5 35.8 %contact_attention.1 = (bf16[384,1024]{1,0:T(8,128)(2,1)}, bf16[384,1024]{1,0:T(8,128)(2,1)}, f32[2,384,1024]{2,1,0:T(8,128)}, bf16[4,2,384,1024]{3,2,1,0:T(8,128)(2,1)}) custom-call(s32[3,6]{1,0:T(4,128)} %broadcast_subtract_fusion.local_ref, s32[3]{0:T(128)} %count_ref.1, bf16[384,1024]{1,0:T(8,128)(2,1)} %q_ref.1, bf16[384,1024]{1,0:T(8,128)(2,1)} %k_ref.3, ...), custom_call_target="tpu_custom_call" | custom-call | tf_op jit(solution)/shard_map/contact_attention/pallas_call | solution.py:291
  109.2 4.5 %fusion.1 = f32[1024,1024]{1,0:T(8,128)} fusion(bf16[384,1024]{1,0:T(8,128)(2,1)} %get-tuple-element.15, bf16[384,1024]{1,0:T(8,128)(2,1)S(1)} %copy-done), kind=kOutput, calls=%fused_computation.7 | convolution fusion | flops 805306368 | bytes 5767168 | tf_op jit(solution)/shard_map/dot_general | solution.py:345
  113.7 0.0 reduce-scatter.2.cloned.1.call-update
  113.7 0.0 copy-start.1
  113.7 0.0 copy-start.4
  113.7 58.2 %return_grads.1 = (bf16[384,1024]{1,0:T(8,128)(2,1)}, bf16[384,1024]{1,0:T(8,128)(2,1)}) custom-call(bf16[4,2,384,1024]{3,2,1,0:T(8,128)(2,1)} %get-tuple-element.17.far, f32[2,384,1024]{2,1,0:T(8,128)} %get-tuple-element.18.own), custom_call_target="tpu_custom_call" | custom-call | bytes 150000000 | tf_op jit(solution)/shard_map/return_grads/pallas_call | solution.py:182
  172.0 0.0 copy-done.1
  172.0 0.0 copy-done.4
  172.0 0.0 copy-start.3
  172.0 1.9 convolution_convert_fusion
  173.8 0.0 copy-start.2
  173.8 23.3 %reduce-scatter.2.cloned.1.call-done = f32[64,1024]{1,0:T(8,128)} async-done(((f32[1024,1024]{1,0:T(8,128)}), f32[64,1024]{1,0:T(8,128)}) %reduce-scatter.2.cloned.1.call-update) | async-done | bytes 262160 | tf_op jit(solution)/shard_map/reduce_scatter | solution.py:344
  197.2 1.7 broadcast_multiply_fusion
  198.8 0.0 copy-done.3
  198.8 0.9 copy.15
  199.7 0.0 copy-done.2
  199.7 0.9 copy.16
Async XLA Ops:
  7.2 61.5 %copy-start = (bf16[384,1024]{1,0:T(8,128)(2,1)S(1)}, bf16[384,1024]{1,0:T(8,128)(2,1)}, u32[]{:S(2)}) copy-start(bf16[384,1024]{1,0:T(8,128)(2,1)} %param.12) | copy-start | bytes 2359300
  7.2 61.5 %all-gather.2.cloned.1.call-start = ((), (), s32[]{:S(2)}) async-start(), calls=%async_computation.1 | async-start | bytes 2228224 | tf_op jit(solution)/shard_map/all_gather | solution.py:326
  7.9 189.3 %reduce-scatter.2.cloned.1.call-start = ((), (), s32[]{:S(2)}) async-start(), calls=%async_computation.2 | async-start | bytes 4456448 | tf_op jit(solution)/shard_map/reduce_scatter | solution.py:344
  113.7 58.3 %copy-start.1 = (bf16[384,1024]{1,0:T(8,128)(2,1)S(1)}, bf16[384,1024]{1,0:T(8,128)(2,1)}, u32[]{:S(2)}) copy-start(bf16[384,1024]{1,0:T(8,128)(2,1)} %get-tuple-element.15) | copy-start | bytes 2359300
  113.7 58.3 %copy-start.4 = (bf16[1024,1024]{1,0:T(8,128)(2,1)S(1)}, bf16[1024,1024]{1,0:T(8,128)(2,1)}, u32[]{:S(2)}) copy-start(bf16[1024,1024]{1,0:T(8,128)(2,1)} %all-gather.2.cloned.1.call-done) | copy-start | bytes 6291460
  172.0 26.9 %copy-start.3 = (bf16[384,1024]{1,0:T(8,128)(2,1)S(1)}, bf16[384,1024]{1,0:T(8,128)(2,1)}, u32[]{:S(2)}) copy-start(bf16[384,1024]{1,0:T(8,128)(2,1)} %get-tuple-element.28) | copy-start | bytes 2359300
  173.8 25.9 %copy-start.2 = (bf16[384,1024]{1,0:T(8,128)(2,1)S(1)}, bf16[384,1024]{1,0:T(8,128)(2,1)}, u32[]{:S(2)}) copy-start(bf16[384,1024]{1,0:T(8,128)(2,1)} %get-tuple-element.29) | copy-start | bytes 2359300
Sparse Core Ops, SparseCore 0:
  10.1 50.0 all-gather.1
  113.8 83.3 reduce-scatter.1
where the time goes:
time: 211 us; the launch traced here: 207 us
  Pallas kernels  151 us (72%)
  waiting for transfers between devices  24 us (11%)
  between operations  14.1 us (7%)
  matrix products  9.8 us (5%)
  local copies, waits for them, and re-layouts  5.26 us (2%)
  other arithmetic  2.94 us (1%)
    pallas_call x1, Pallas kernels, return_grads(): pl.pallas_call(functools.partial(return_kernel, n, chunks), out_shape=[sh...  58.2 us
    pallas_call x1, Pallas kernels, gather_window(): pl.pallas_call(functools.partial(gather_kernel, n, chunks), out_shape=[sh...  57.3 us
    pallas_call x1, Pallas kernels, attention(): pl.pallas_call(functools.partial(attention_kernel, blocks, listed, block,...  35.8 us
    reduce_scatter x1, waiting for transfers between devices, shards(): lax.psum_scatter(lax.dot_general(attended, grad_output, (((0,), (0,)), ((...  23.3 us
    dot_general x1, matrix products, shards(): lax.dot_general(attended, grad_output, (((0,), (0,)), ((), ())), preferre...  4.46 us
  transfers between devices with their start and end apart: 2, of which 1 were waited for; matrix products, arithmetic and copies ran while one was open for 3% of the time, Pallas kernels for 56%

commit v1 on v0

--- a/solution.py
+++ b/solution.py
@@ -342,11 +342,11 @@
     grad_keys, grad_values = return_grads(far, own)
     mixed = jnp.dot(attended, weight, preferred_element_type=f32).astype(bf16)
     grad_weight = lax.psum_scatter(
-        lax.dot_general(attended, grad_output, (((0,), (0,)), ((), ())), preferred_element_type=f32),
+        lax.dot_general(attended, grad_output, (((0,), (0,)), ((), ())), preferred_element_type=f32).astype(bf16),
         "ctx",
         scatter_dimension=0,
         tiled=True,
-    ) * jnp.float32(1.0 / math.sqrt(total_tokens))
+    ).astype(f32) * jnp.float32(1.0 / math.sqrt(total_tokens))
     return mixed, grad_queries, grad_keys, grad_values, grad_weight
 
 

time: 211 us -> 193 us (0.915)
  waiting for transfers between devices: 24 us -> 10.4 us
    reduce_scatter x1, waiting for transfers between devices: 23.3 us -> 9.7 us  [shards(): lax.psum_scatter(lax.dot_general(attended, grad_output, (((0,), (0,)), ((...]
    pallas_call x1, Pallas kernels: 58.2 us -> 55.5 us  [return_grads(): pl.pallas_call(functools.partial(return_kernel, n, chunks), out_shape=[sh...]
  transfers between devices with their start and end apart: 2 -> 2, of which waited for: 1 -> 1; matrix products, arithmetic and copies ran while one was open for 3% -> 3% of each run, Pallas kernels for 56% -> 59%
where the time goes in v1:
time: 193 us; the launch traced here: 190 us
  Pallas kernels  149 us (77%)
  between operations  14.1 us (7%)
  waiting for transfers between devices  10.4 us (5%)
  matrix products  9.07 us (5%)
  local copies, waits for them, and re-layouts  5.26 us (3%)
  other arithmetic  2.89 us (1%)
    pallas_call x1, Pallas kernels, gather_window(): pl.pallas_call(functools.partial(gather_kernel, n, chunks), out_shape=[sh...  57.3 us
    pallas_call x1, Pallas kernels, return_grads(): pl.pallas_call(functools.partial(return_kernel, n, chunks), out_shape=[sh...  55.5 us
    pallas_call x1, Pallas kernels, attention(): pl.pallas_call(functools.partial(attention_kernel, blocks, listed, block,...  35.7 us
    reduce_scatter x1, waiting for transfers between devices, shards(): lax.psum_scatter(lax.dot_general(attended, grad_output, (((0,), (0,)), ((...  9.7 us
  transfers between devices with their start and end apart: 2, of which 1 were waited for; matrix products, arithmetic and copies ran while one was open for 3% of the time, Pallas kernels for 59%

profile of v1, /device:TPU:20, one launch (start us, length us, event | category | flops | bytes accessed | tf_op | source)
XLA Modules:
  0.0 190.3 jit_solution(12227510440370093366)
XLA Ops:
  7.2 0.0 copy-start
  7.2 0.0 all-gather.2.cloned.1.call-start
  7.2 0.7 all-gather.2.cloned.1.call-update
  7.9 0.0 reduce-scatter.2.cloned.1.call-start
  8.0 57.3 %gather_window.1 = (bf16[4,384,1024]{2,1,0:T(8,128)(2,1)}, bf16[4,384,1024]{2,1,0:T(8,128)(2,1)}) custom-call(bf16[384,1024]{1,0:T(8,128)(2,1)} %k_ref.3, bf16[384,1024]{1,0:T(8,128)(2,1)} %v_ref.3), custom_call_target="tpu_custom_call" | custom-call | bytes 150000000 | tf_op jit(solution)/shard_map/gather_window/pallas_call | solution.py:101
  65.2 1.4 fusion.idq_ref
  66.6 0.8 pad_dynamic-slice_fusion.1
  67.4 1.3 broadcast_subtract_fusion.local_ref
  68.6 0.0 all-gather.2.cloned.1.call-done
  68.6 0.0 copy-done
  68.7 3.5 %convolution_convert_fusion.2.d_ref = bf16[384,1024]{1,0:T(8,128)(2,1)} fusion(bf16[384,1024]{1,0:T(8,128)(2,1)S(1)} %copy-done, bf16[1024,1024]{1,0:T(8,128)(2,1)} %all-gather.2.cloned.1.call-done), kind=kOutput, calls=%fused_computation.2 | convolution fusion | flops 805699584 | bytes 3670016 | tf_op jit(solution)/shard_map/dot_general | solution.py:328
  72.1 1.3 broadcast_in_dim.2.idk_ref
  73.5 35.7 %contact_attention.1 = (bf16[384,1024]{1,0:T(8,128)(2,1)}, bf16[384,1024]{1,0:T(8,128)(2,1)}, f32[2,384,1024]{2,1,0:T(8,128)}, bf16[4,2,384,1024]{3,2,1,0:T(8,128)(2,1)}) custom-call(s32[3,6]{1,0:T(4,128)} %broadcast_subtract_fusion.local_ref, s32[3]{0:T(128)} %count_ref.1, bf16[384,1024]{1,0:T(8,128)(2,1)} %q_ref.1, bf16[384,1024]{1,0:T(8,128)(2,1)} %k_ref.3, ...), custom_call_target="tpu_custom_call" | custom-call | tf_op jit(solution)/shard_map/contact_attention/pallas_call | solution.py:291
  109.2 3.7 %convolution_convert_fusion = bf16[1024,1024]{1,0:T(8,128)(2,1)} fusion(bf16[384,1024]{1,0:T(8,128)(2,1)} %get-tuple-element.15, bf16[384,1024]{1,0:T(8,128)(2,1)S(1)} %copy-done), kind=kOutput, calls=%fused_computation | convolution fusion | flops 806354944 | bytes 3670016 | tf_op jit(solution)/shard_map/dot_general | solution.py:345
  112.9 0.0 reduce-scatter.2.cloned.1.call-update
  112.9 0.0 copy-start.3
  112.9 0.0 copy-start.4
  113.0 55.5 %return_grads.1 = (bf16[384,1024]{1,0:T(8,128)(2,1)}, bf16[384,1024]{1,0:T(8,128)(2,1)}) custom-call(bf16[4,2,384,1024]{3,2,1,0:T(8,128)(2,1)} %get-tuple-element.17.far, f32[2,384,1024]{2,1,0:T(8,128)} %get-tuple-element.18.own), custom_call_target="tpu_custom_call" | custom-call | bytes 150000000 | tf_op jit(solution)/shard_map/return_grads/pallas_call | solution.py:182
  168.5 0.0 copy-done.3
  168.5 0.0 copy-done.4
  168.5 0.0 copy-start.2
  168.5 1.9 convolution_convert_fusion.1
  170.4 0.0 copy-start.1
  170.4 9.7 %reduce-scatter.2.cloned.1.call-done = bf16[64,1024]{1,0:T(8,128)(2,1)} async-done(((bf16[1024,1024]{1,0:T(8,128)(2,1)}), bf16[64,1024]{1,0:T(8,128)(2,1)}) %reduce-scatter.2.cloned.1.call-update) | async-done | bytes 131088 | tf_op jit(solution)/shard_map/reduce_scatter | solution.py:344
  180.1 1.6 convert_multiply_fusion
  181.7 0.0 copy-done.2
  181.7 0.9 copy.15
  182.6 0.0 copy-done.1
  182.6 0.9 copy.16
Async XLA Ops:
  7.2 61.5 %copy-start = (bf16[384,1024]{1,0:T(8,128)(2,1)S(1)}, bf16[384,1024]{1,0:T(8,128)(2,1)}, u32[]{:S(2)}) copy-start(bf16[384,1024]{1,0:T(8,128)(2,1)} %param.12) | copy-start | bytes 2359300
  7.2 61.5 %all-gather.2.cloned.1.call-start = ((), (), s32[]{:S(2)}) async-start(), calls=%async_computation.1 | async-start | bytes 2228224 | tf_op jit(solution)/shard_map/all_gather | solution.py:326
  7.9 172.2 %reduce-scatter.2.cloned.1.call-start = ((), (), s32[]{:S(2)}) async-start(), calls=%async_computation.2 | async-start | bytes 2228224 | tf_op jit(solution)/shard_map/reduce_scatter | solution.py:344
  112.9 55.6 %copy-start.3 = (bf16[1024,1024]{1,0:T(8,128)(2,1)S(1)}, bf16[1024,1024]{1,0:T(8,128)(2,1)}, u32[]{:S(2)}) copy-start(bf16[1024,1024]{1,0:T(8,128)(2,1)} %all-gather.2.cloned.1.call-done) | copy-start | bytes 6291460
  112.9 55.6 %copy-start.4 = (bf16[384,1024]{1,0:T(8,128)(2,1)S(1)}, bf16[384,1024]{1,0:T(8,128)(2,1)}, u32[]{:S(2)}) copy-start(bf16[384,1024]{1,0:T(8,128)(2,1)} %get-tuple-element.15) | copy-start | bytes 2359300
  168.5 13.2 %copy-start.2 = (bf16[384,1024]{1,0:T(8,128)(2,1)S(1)}, bf16[384,1024]{1,0:T(8,128)(2,1)}, u32[]{:S(2)}) copy-start(bf16[384,1024]{1,0:T(8,128)(2,1)} %get-tuple-element.28) | copy-start | bytes 2359300
  170.4 12.2 %copy-start.1 = (bf16[384,1024]{1,0:T(8,128)(2,1)S(1)}, bf16[384,1024]{1,0:T(8,128)(2,1)}, u32[]{:S(2)}) copy-start(bf16[384,1024]{1,0:T(8,128)(2,1)} %get-tuple-element.29) | copy-start | bytes 2359300
Sparse Core Ops, SparseCore 0:
  10.1 50.0 all-gather.1
  113.1 66.9 reduce-scatter.1

commit v2 on v1

--- a/solution.py
+++ b/solution.py
@@ -94,7 +94,7 @@
         pl.when((y != core) | has_behind)(lambda c=c: onward(c).wait_recv())
 
 
-def gather_window(keys, values, chunks=6):
+def gather_window(keys, values, chunks=12):
     n = lax.axis_size("ctx")
     any_space = pl.BlockSpec(memory_space=pl.ANY)
     shape = jax.ShapeDtypeStruct((2 * REACH_DEV,) + keys.shape, keys.dtype)
@@ -174,7 +174,7 @@
         over_y(c).wait_send()
 
 
-def return_grads(far, own, chunks=6):
+def return_grads(far, own, chunks=12):
     n = lax.axis_size("ctx")
     _, rows, width = own.shape
     space = pl.BlockSpec(memory_space=pltpu.VMEM)

time: 193 us -> 195 us (1.010)
  Pallas kernels: 149 us -> 151 us
    pallas_call x1, Pallas kernels: 55.5 us -> 58.2 us  [return_grads(): pl.pallas_call(functools.partial(return_kernel, n, chunks), out_shape=[sh...]
  transfers between devices with their start and end apart: 2 -> 2, of which waited for: 1 -> 1; matrix products, arithmetic and copies ran while one was open for 3% -> 3% of each run, Pallas kernels for 59% -> 60%
where the time goes in v2:
time: 195 us; the launch traced here: 192 us
  Pallas kernels  151 us (77%)
  between operations  14.1 us (7%)
  waiting for transfers between devices  9.93 us (5%)
  matrix products  9.07 us (5%)
  local copies, waits for them, and re-layouts  5.26 us (3%)
  other arithmetic  2.89 us (1%)
    pallas_call x1, Pallas kernels, return_grads(): pl.pallas_call(functools.partial(return_kernel, n, chunks), out_shape=[sh...  58.2 us
    pallas_call x1, Pallas kernels, gather_window(): pl.pallas_call(functools.partial(gather_kernel, n, chunks), out_shape=[sh...  56.6 us
    pallas_call x1, Pallas kernels, attention(): pl.pallas_call(functools.partial(attention_kernel, blocks, listed, block,...  35.7 us
    reduce_scatter x1, waiting for transfers between devices, shards(): lax.psum_scatter(lax.dot_general(attended, grad_output, (((0,), (0,)), ((...  9.23 us
  transfers between devices with their start and end apart: 2, of which 1 were waited for; matrix products, arithmetic and copies ran while one was open for 3% of the time, Pallas kernels for 60%

profile of v2, /device:TPU:20, one launch (start us, length us, event | category | flops | bytes accessed | tf_op | source)
XLA Modules:
  0.0 191.9 jit_solution(2083574863746133754)
XLA Ops:
  7.2 0.0 copy-start
  7.2 0.0 all-gather.2.cloned.1.call-start
  7.2 0.7 all-gather.2.cloned.1.call-update
  7.9 0.0 reduce-scatter.2.cloned.1.call-start
  8.0 56.6 %gather_window.1 = (bf16[4,384,1024]{2,1,0:T(8,128)(2,1)}, bf16[4,384,1024]{2,1,0:T(8,128)(2,1)}) custom-call(bf16[384,1024]{1,0:T(8,128)(2,1)} %k_ref.3, bf16[384,1024]{1,0:T(8,128)(2,1)} %v_ref.3), custom_call_target="tpu_custom_call" | custom-call | bytes 150000000 | tf_op jit(solution)/shard_map/gather_window/pallas_call | solution.py:101
  64.6 1.4 fusion.idq_ref
  66.0 0.8 pad_dynamic-slice_fusion.1
  66.8 1.3 broadcast_subtract_fusion.local_ref
  68.0 0.0 all-gather.2.cloned.1.call-done
  68.0 0.0 copy-done
  68.0 3.5 %convolution_convert_fusion.2.d_ref = bf16[384,1024]{1,0:T(8,128)(2,1)} fusion(bf16[384,1024]{1,0:T(8,128)(2,1)S(1)} %copy-done, bf16[1024,1024]{1,0:T(8,128)(2,1)} %all-gather.2.cloned.1.call-done), kind=kOutput, calls=%fused_computation.2 | convolution fusion | flops 805699584 | bytes 3670016 | tf_op jit(solution)/shard_map/dot_general | solution.py:328
  71.5 1.3 broadcast_in_dim.2.idk_ref
  72.8 35.7 %contact_attention.1 = (bf16[384,1024]{1,0:T(8,128)(2,1)}, bf16[384,1024]{1,0:T(8,128)(2,1)}, f32[2,384,1024]{2,1,0:T(8,128)}, bf16[4,2,384,1024]{3,2,1,0:T(8,128)(2,1)}) custom-call(s32[3,6]{1,0:T(4,128)} %broadcast_subtract_fusion.local_ref, s32[3]{0:T(128)} %count_ref.1, bf16[384,1024]{1,0:T(8,128)(2,1)} %q_ref.1, bf16[384,1024]{1,0:T(8,128)(2,1)} %k_ref.3, ...), custom_call_target="tpu_custom_call" | custom-call | tf_op jit(solution)/shard_map/contact_attention/pallas_call | solution.py:291
  108.6 3.7 %convolution_convert_fusion = bf16[1024,1024]{1,0:T(8,128)(2,1)} fusion(bf16[384,1024]{1,0:T(8,128)(2,1)} %get-tuple-element.15, bf16[384,1024]{1,0:T(8,128)(2,1)S(1)} %copy-done), kind=kOutput, calls=%fused_computation | convolution fusion | flops 806354944 | bytes 3670016 | tf_op jit(solution)/shard_map/dot_general | solution.py:345
  112.3 0.0 reduce-scatter.2.cloned.1.call-update
  112.3 0.0 copy-start.3
  112.3 0.0 copy-start.4
  112.3 58.2 %return_grads.1 = (bf16[384,1024]{1,0:T(8,128)(2,1)}, bf16[384,1024]{1,0:T(8,128)(2,1)}) custom-call(bf16[4,2,384,1024]{3,2,1,0:T(8,128)(2,1)} %get-tuple-element.17.far, f32[2,384,1024]{2,1,0:T(8,128)} %get-tuple-element.18.own), custom_call_target="tpu_custom_call" | custom-call | bytes 150000000 | tf_op jit(solution)/shard_map/return_grads/pallas_call | solution.py:182
  170.5 0.0 copy-done.3
  170.5 0.0 copy-done.4
  170.5 0.0 copy-start.2
  170.6 1.9 convolution_convert_fusion.1
  172.4 0.0 copy-start.1
  172.4 9.2 %reduce-scatter.2.cloned.1.call-done = bf16[64,1024]{1,0:T(8,128)(2,1)} async-done(((bf16[1024,1024]{1,0:T(8,128)(2,1)}), bf16[64,1024]{1,0:T(8,128)(2,1)}) %reduce-scatter.2.cloned.1.call-update) | async-done | bytes 131088 | tf_op jit(solution)/shard_map/reduce_scatter | solution.py:344
  181.7 1.6 convert_multiply_fusion
  183.3 0.0 copy-done.2
  183.3 0.9 copy.15
  184.2 0.0 copy-done.1
  184.2 0.9 copy.16
Async XLA Ops:
  7.2 60.9 %copy-start = (bf16[384,1024]{1,0:T(8,128)(2,1)S(1)}, bf16[384,1024]{1,0:T(8,128)(2,1)}, u32[]{:S(2)}) copy-start(bf16[384,1024]{1,0:T(8,128)(2,1)} %param.12) | copy-start | bytes 2359300
  7.2 60.8 %all-gather.2.cloned.1.call-start = ((), (), s32[]{:S(2)}) async-start(), calls=%async_computation.1 | async-start | bytes 2228224 | tf_op jit(solution)/shard_map/all_gather | solution.py:326
  7.9 173.7 %reduce-scatter.2.cloned.1.call-start = ((), (), s32[]{:S(2)}) async-start(), calls=%async_computation.2 | async-start | bytes 2228224 | tf_op jit(solution)/shard_map/reduce_scatter | solution.py:344
  112.3 58.2 %copy-start.3 = (bf16[1024,1024]{1,0:T(8,128)(2,1)S(1)}, bf16[1024,1024]{1,0:T(8,128)(2,1)}, u32[]{:S(2)}) copy-start(bf16[1024,1024]{1,0:T(8,128)(2,1)} %all-gather.2.cloned.1.call-done) | copy-start | bytes 6291460
  112.3 58.2 %copy-start.4 = (bf16[384,1024]{1,0:T(8,128)(2,1)S(1)}, bf16[384,1024]{1,0:T(8,128)(2,1)}, u32[]{:S(2)}) copy-start(bf16[384,1024]{1,0:T(8,128)(2,1)} %get-tuple-element.15) | copy-start | bytes 2359300
  170.5 12.7 %copy-start.2 = (bf16[384,1024]{1,0:T(8,128)(2,1)S(1)}, bf16[384,1024]{1,0:T(8,128)(2,1)}, u32[]{:S(2)}) copy-start(bf16[384,1024]{1,0:T(8,128)(2,1)} %get-tuple-element.28) | copy-start | bytes 2359300
  172.4 11.7 %copy-start.1 = (bf16[384,1024]{1,0:T(8,128)(2,1)S(1)}, bf16[384,1024]{1,0:T(8,128)(2,1)}, u32[]{:S(2)}) copy-start(bf16[384,1024]{1,0:T(8,128)(2,1)} %get-tuple-element.29) | copy-start | bytes 2359300
Sparse Core Ops, SparseCore 0:
  10.1 50.0 all-gather.1
  112.4 69.1 reduce-scatter.1
